TPU v7x, 32 devices: a whole 2x2x4 slice. The times are simulated.
32 devices in a mesh: rows: 8 (over y, x, core), depth: 4 (over z).
Axes of the slice: x: 2, y: 2, z: 4, core: 2. Of those that a mesh axis runs over, the one named last changes fastest.
Arguments:
- left_factors: bfloat16 [8, 8, 2048, 128], P('rows', 'depth'), may hold values from -0.125 to 0.125
- right_factors: bfloat16 [8, 8, 2048, 128], P('rows', 'depth'), may hold values from -0.125 to 0.125
- probe_matrix: bfloat16 [2048, 128], replicated, may hold values from -6 to 6
- tile_list: int32 [8, 4], replicated, may hold values from 0 to 7, all different within a row
Outputs:
- basis: float32 [8, 4, 2048, 128], P('rows', None, 'depth')
- chol_factor: float32 [8, 4, 128, 128], P('rows')
Inputs may be any that keep to these rules, and one draw needn't show every extreme that they name: `tile_list`: each row holds 4 different tile rows, and every tile row is named by some row.
All inputs are finite; a program needn't handle non-finite values.
Results may differ from a plain program's by a relative error of at most 0.0058.
Values may be sent and summed in bfloat16 or wider, within the bound.
No kernel may reach another device: no remote copies, remote signals or barrier semaphores. Data moves between devices by JAX's collectives and lax.ppermute only.
A program may use at most 64 MiB of HBM per device.

v0:
```python
import math
import jax
import jax.numpy as jnp
from jax import lax
from jax.sharding import PartitionSpec as P


def on_device(left_factors, right_factors, probe_matrix, tile_list):
    left_own = left_factors[0]
    right_own = right_factors[0]
    panels, tile_size, rank_size = left_own.shape
    scale = math.sqrt(float(tile_size))
    image = jnp.einsum(
        "pbk,bl->pkl", left_own, probe_matrix, preferred_element_type=jnp.float32
    ).astype(jnp.bfloat16)
    sketch_rows = jnp.einsum(
        "pbk,pkl->pbl", right_own, image, preferred_element_type=jnp.float32
    ).astype(jnp.bfloat16)
    sliced = lax.all_to_all(sketch_rows[:, None], "rows", split_axis=2, concat_axis=1, tiled=True)
    readers_order = jnp.transpose(tile_list)
    outgoing = jnp.take(sliced, readers_order, axis=1)
    arrived = lax.all_to_all(outgoing, "rows", split_axis=2, concat_axis=2, tiled=True)
    listed = arrived.shape[1]
    arrived = arrived.reshape(panels, listed, tile_size, rank_size)
    coupling = jnp.einsum(
        "pbk,ptbl->tpkl", right_own, arrived, preferred_element_type=jnp.float32
    ).astype(jnp.bfloat16)
    partial_sketch = jnp.einsum(
        "pbk,tpkl->tbl", left_own, coupling, preferred_element_type=jnp.float32
    )
    own_rows = lax.psum_scatter(partial_sketch, "depth", scatter_dimension=1, tiled=True)
    gram_part = jnp.einsum("tbk,tbl->tkl", own_rows, own_rows, precision=lax.Precision.HIGHEST)
    gram = lax.psum(gram_part, "depth")
    lower = jnp.linalg.cholesky(gram)
    solved = jax.scipy.linalg.solve_triangular(
        lower, jnp.transpose(own_rows, (0, 2, 1)), lower=True
    )
    basis = jnp.transpose(solved, (0, 2, 1)) * scale
    return (basis[None], (lower / scale)[None])


def solution(mesh):
    in_specs = (P("rows", "depth", None, None), P("rows", "depth", None, None), P(), P())
    out_specs = (P("rows", None, "depth", None), P("rows", None, None, None))
    return jax.shard_map(
        on_device, mesh=mesh, in_specs=in_specs, out_specs=out_specs, check_vma=False
    )
```

profile of v0, /device:TPU:0, one launch (start us, length us, event | category | flops | bytes accessed | tf_op | source)
XLA Modules:
  0.0 313.9 jit_solution(2542688194420749601)
XLA Ops:
  7.2 1.2 copy-done
  8.4 2.3 fusion.3
  10.7 2.0 copy.43
  12.7 5.2 %all-to-all-start = ((bf16[2,1,2048,128]{3,0,1,2:T(2,128)(2,1)}), bf16[2,1,2048,128]{3,0,1,2:T(2,128)(2,1)S(1)}, u32[]{:S(2)}, u32[]{:S(2)}) async-start(bf16[2,1,2048,128]{3,0,1,2:T(2,128)(2,1)} %copy.43), calls=%async_computation | async-start | bytes 2097152 | tf_op jit(solution)/shard_map/all_to_all | solution.py:19
  18.0 0.1 reshape.29
  18.0 0.1 copy.40
  18.2 15.1 %all-to-all-done = bf16[2,1,2048,128]{3,0,1,2:T(2,128)(2,1)S(1)} async-done(((bf16[2,1,2048,128]{3,0,1,2:T(2,128)(2,1)}), bf16[2,1,2048,128]{3,0,1,2:T(2,128)(2,1)S(1)}, u32[]{:S(2)}, u32[]{:S(2)}) %all-to-all-start) | async-done | bytes 1048608 | tf_op jit(solution)/shard_map/all_to_all | solution.py:19
  33.3 0.1 copy.44
  33.4 3.0 gather_fusion
  36.4 2.6 fusion.2
  39.1 51.5 %all_to_all.17 = bf16[2,4,8,256,128]{4,3,1,0,2:T(8,128)(2,1)S(1)} all-to-all(bf16[2,4,8,256,128]{4,3,1,0,2:T(8,128)(2,1)S(1)} %fusion.2), channel_id=1, replica_groups=mesh['rows'=8,'depth'=4] {'rows'}, dimensions={2} | all-to-all | bytes 8388608 | tf_op jit(solution)/shard_map/all_to_all | solution.py:22
  90.6 2.2 copy.46
  92.9 6.1 %convolution_bitcast_fusion = f32[4,2048,128]{1,2,0:T(8,128)} fusion(bf16[1,2,2048,128]{3,2,1,0:T(8,128)(2,1)S(1)} %copy-done, bf16[2,4,2048,128]{3,2,1,0:T(8,128)(2,1)} %bitcast.59, bf16[1,2,2048,128]{3,2,1,0:T(8,128)(2,1)S(1)} %copy-done.2), kind=kOutput, calls=%fused_computation.5 | convolution fusion | flops 1073872896 | bytes 10485760 | tf_op jit(solution)/shard_map/pbk,tpkl->tbl/dot_general | solution.py:28
  99.0 0.2 all-reduce.2.cloned.1.call-start
  99.2 76.1 %reduce-scatter.2.cloned.1.call-done = f32[4,512,128]{1,2,0:T(8,128)} async-done(((f32[4,2048,128]{1,2,0:T(8,128)}), f32[4,512,128]{1,2,0:T(8,128)}) %reduce-scatter.2.cloned.1.call-update) | async-done | bytes 1048592 | tf_op jit(solution)/shard_map/reduce_scatter | solution.py:31
  175.3 3.5 %fusion.24 = f32[4,128,128]{1,2,0:T(8,128)} fusion(f32[4,512,128]{1,2,0:T(8,128)} %reduce-scatter.2.cloned.1.call-done), kind=kOutput, calls=%fused_computation.31 | convolution fusion | flops 402653184 | bytes 1310720 | tf_op jit(solution)/shard_map/tbk,tbl->tkl/dot_general | solution.py:32
  178.9 36.2 %all-reduce.2.cloned.1.call-done = f32[4,128,128]{1,2,0:T(8,128)} async-done(((f32[4,128,128]{1,2,0:T(8,128)}), f32[4,128,128]{1,2,0:T(8,128)}) %all-reduce.2.cloned.1.call-update) | async-done | bytes 262160 | tf_op jit(solution)/shard_map/psum | solution.py:33
  215.1 1.1 copy.50
  216.1 1.0 fusion.23
  217.1 46.9 %custom-call.8 = f32[4,128,128]{2,1,0:T(8,128)S(1)} custom-call(f32[4,128,128]{2,1,0:T(8,128)S(1)} %fusion.23), custom_call_target="Cholesky" | custom-call | tf_op jit(solution)/shard_map/jit(cholesky)/cholesky | solution.py:34
  264.1 0.1 compare_reduce_fusion
  264.2 0.8 multiply_bitcast_fusion
  265.0 39.3 %custom-call.9 = f32[4,1,128,128]{2,3,1,0:T(8,128)S(1)} custom-call(f32[4,1,128,128]{3,2,1,0:T(8,128)S(1)} %get-tuple-element.3), custom_call_target="InvertDiagBlocksLowerTriangular" | custom-call | tf_op jit(solution)/shard_map/jit(_solve_triangular)/vmap()/triangular_solve | solution.py:35
  304.3 2.8 fusion.4
  (16 shorter events, 0.2 us)
Async XLA Ops:
  7.2 1.2 copy-start
  8.4 9.5 %copy-start.3 = (s32[8,4]{0,1:T(4,128)S(1)}, s32[8,4]{0,1:T(4,128)}, u32[]{:S(2)}) copy-start(s32[8,4]{0,1:T(4,128)} %param.7) | copy-start | bytes 388
  12.7 20.6 %all-to-all-start = ((bf16[2,1,2048,128]{3,0,1,2:T(2,128)(2,1)}), bf16[2,1,2048,128]{3,0,1,2:T(2,128)(2,1)S(1)}, u32[]{:S(2)}, u32[]{:S(2)}) async-start(bf16[2,1,2048,128]{3,0,1,2:T(2,128)(2,1)} %copy.43), calls=%async_computation | async-start | bytes 2097152 | tf_op jit(solution)/shard_map/all_to_all | solution.py:19
  17.9 157.4 %reduce-scatter.2.cloned.1.call-start = ((), (), s32[]{:S(2)}) async-start(), calls=%async_computation.3 | async-start | bytes 5242880 | tf_op jit(solution)/shard_map/reduce_scatter | solution.py:31
  90.6 2.2 copy-start.2
  99.0 116.0 %all-reduce.2.cloned.1.call-start = ((), (), s32[]{:S(2)}) async-start(), calls=%async_computation.4 | async-start | bytes 524288 | tf_op jit(solution)/shard_map/psum | solution.py:33
  175.3 129.0 %copy-start.1 = (f32[4,512,128]{1,2,0:T(8,128)S(1)}, f32[4,512,128]{1,2,0:T(8,128)}, u32[]{:S(2)}) copy-start(f32[4,512,128]{1,2,0:T(8,128)} %reduce-scatter.2.cloned.1.call-done) | copy-start | bytes 3145732
Sparse Core Ops, SparseCore 0:
  99.1 76.1 reduce-scatter.1
  178.9 36.0 all-reduce.1
where the time goes:
time: 314 us
  waiting for transfers between devices  127 us (40%)
  other arithmetic  90.9 us (29%)
  blocking collectives  51.5 us (16%)
  matrix products  14.7 us (5%)
  between operations  14.1 us (4%)
  local copies, waits for them, and re-layouts  9.88 us (3%)
  starting transfers between devices  5.46 us (2%)
    reduce_scatter x1, waiting for transfers between devices, on_device(): lax.psum_scatter(partial_sketch, 'depth', scatter_dimension=1, tiled=True)  76.1 us
    all_to_all x1, blocking collectives, on_device(): lax.all_to_all(outgoing, 'rows', split_axis=2, concat_axis=2, tiled=True)  51.5 us
    another operation x4, other arithmetic, on_device(): lower = jnp.linalg.cholesky(gram)  47.1 us
    another operation x2, other arithmetic, on_device(): jax.scipy.linalg.solve_triangular(lower, jnp.transpose(own_rows, (0, 2, 1...  39.3 us
    psum x1, waiting for transfers between devices, on_device(): gram = lax.psum(gram_part, 'depth')  36.2 us
    all_to_all x1, waiting for transfers between devices, on_device(): lax.all_to_all(sketch_rows[:, None], 'rows', split_axis=2, concat_axis=1,...  15.1 us
  transfers between devices with their start and end apart: 3, of which 3 were waited for; matrix products, arithmetic and copies ran while one was open for 0% of the time, Pallas kernels for 0%

commit v1 on v0

--- a/solution.py
+++ b/solution.py
@@ -30,7 +30,7 @@
     )
     own_rows = lax.psum_scatter(partial_sketch, "depth", scatter_dimension=1, tiled=True)
     gram_part = jnp.einsum("tbk,tbl->tkl", own_rows, own_rows, precision=lax.Precision.HIGHEST)
-    gram = lax.psum(gram_part, "depth")
+    gram = jnp.sum(lax.all_gather(gram_part, "depth"), axis=0)
     lower = jnp.linalg.cholesky(gram)
     solved = jax.scipy.linalg.solve_triangular(
         lower, jnp.transpose(own_rows, (0, 2, 1)), lower=True

time: 314 us -> 306 us (0.975)
  waiting for transfers between devices: 127 us -> 120 us
    psum x1 -> x0, waiting for transfers between devices: 36.2 us -> none  [on_device(): gram = lax.psum(gram_part, 'depth')]
    all_gather x0 -> x1, waiting for transfers between devices: none -> 28.6 us  [on_device(): gram = jnp.sum(lax.all_gather(gram_part, 'depth'), axis=0)]
where the time goes in v1:
time: 306 us
  waiting for transfers between devices  120 us (39%)
  other arithmetic  91.2 us (30%)
  blocking collectives  51.5 us (17%)
  matrix products  14.6 us (5%)
  between operations  14.1 us (5%)
  local copies, waits for them, and re-layouts  8.93 us (3%)
  starting transfers between devices  5.46 us (2%)
    reduce_scatter x1, waiting for transfers between devices, on_device(): lax.psum_scatter(partial_sketch, 'depth', scatter_dimension=1, tiled=True)  76.1 us
    all_to_all x1, blocking collectives, on_device(): lax.all_to_all(outgoing, 'rows', split_axis=2, concat_axis=2, tiled=True)  51.5 us
    another operation x4, other arithmetic, on_device(): lower = jnp.linalg.cholesky(gram)  47.1 us
    another operation x2, other arithmetic, on_device(): jax.scipy.linalg.solve_triangular(lower, jnp.transpose(own_rows, (0, 2, 1...  39.3 us
    all_gather x1, waiting for transfers between devices, on_device(): gram = jnp.sum(lax.all_gather(gram_part, 'depth'), axis=0)  28.6 us
    all_to_all x1, waiting for transfers between devices, on_device(): lax.all_to_all(sketch_rows[:, None], 'rows', split_axis=2, concat_axis=1,...  15.1 us
    dot_general x1, matrix products, on_device(): jnp.einsum('pbk,tpkl->tbl', left_own, coupling, preferred_element_type=jn...  6.14 us
  transfers between devices with their start and end apart: 3, of which 3 were waited for; matrix products, arithmetic and copies ran while one was open for 0% of the time, Pallas kernels for 0%

profile of v1, /device:TPU:0, one launch (start us, length us, event | category | flops | bytes accessed | tf_op | source)
XLA Modules:
  0.0 305.7 jit_solution(12468124127899089897)
XLA Ops:
  7.2 1.2 copy-done
  8.4 2.3 fusion.3
  10.7 2.0 copy.39
  12.7 5.2 %all-to-all-start = ((bf16[2,1,2048,128]{3,0,1,2:T(2,128)(2,1)}), bf16[2,1,2048,128]{3,0,1,2:T(2,128)(2,1)S(1)}, u32[]{:S(2)}, u32[]{:S(2)}) async-start(bf16[2,1,2048,128]{3,0,1,2:T(2,128)(2,1)} %copy.39), calls=%async_computation | async-start | bytes 2097152 | tf_op jit(solution)/shard_map/all_to_all | solution.py:19
  18.0 0.1 reshape.29
  18.0 0.1 copy.36
  18.2 15.1 %all-to-all-done = bf16[2,1,2048,128]{3,0,1,2:T(2,128)(2,1)S(1)} async-done(((bf16[2,1,2048,128]{3,0,1,2:T(2,128)(2,1)}), bf16[2,1,2048,128]{3,0,1,2:T(2,128)(2,1)S(1)}, u32[]{:S(2)}, u32[]{:S(2)}) %all-to-all-start) | async-done | bytes 1048608 | tf_op jit(solution)/shard_map/all_to_all | solution.py:19
  33.3 0.1 copy.40
  33.4 3.0 gather_fusion
  36.4 2.6 fusion.2
  39.1 51.5 %all_to_all.17 = bf16[2,4,8,256,128]{4,3,1,0,2:T(8,128)(2,1)S(1)} all-to-all(bf16[2,4,8,256,128]{4,3,1,0,2:T(8,128)(2,1)S(1)} %fusion.2), channel_id=1, replica_groups=mesh['rows'=8,'depth'=4] {'rows'}, dimensions={2} | all-to-all | bytes 8388608 | tf_op jit(solution)/shard_map/all_to_all | solution.py:22
  90.6 2.2 copy.42
  92.9 6.1 %convolution_bitcast_fusion = f32[4,2048,128]{1,2,0:T(8,128)} fusion(bf16[1,2,2048,128]{3,2,1,0:T(8,128)(2,1)S(1)} %copy-done, bf16[2,4,2048,128]{3,2,1,0:T(8,128)(2,1)} %bitcast.60, bf16[1,2,2048,128]{3,2,1,0:T(8,128)(2,1)S(1)} %copy-done.2), kind=kOutput, calls=%fused_computation.5 | convolution fusion | flops 1073872896 | bytes 10485760 | tf_op jit(solution)/shard_map/pbk,tpkl->tbl/dot_general | solution.py:28
  99.0 0.2 all-gather.3.cloned.1.call-start
  99.2 76.1 %reduce-scatter.2.cloned.1.call-done = f32[4,512,128]{1,2,0:T(8,128)} async-done(((f32[4,2048,128]{1,2,0:T(8,128)}), f32[4,512,128]{1,2,0:T(8,128)}) %reduce-scatter.2.cloned.1.call-update) | async-done | bytes 1048592 | tf_op jit(solution)/shard_map/reduce_scatter | solution.py:31
  175.3 3.4 %fusion.24 = f32[4,128,128]{2,1,0:T(8,128)} fusion(f32[4,512,128]{1,2,0:T(8,128)} %reduce-scatter.2.cloned.1.call-done), kind=kOutput, calls=%fused_computation.31 | convolution fusion | flops 402653184 | bytes 1310720 | tf_op jit(solution)/shard_map/tbk,tbl->tkl/dot_general | solution.py:32
  178.8 28.6 %all-gather.3.cloned.1.call-done = f32[16,128,128]{2,1,0:T(8,128)} async-done(((f32[4,128,128]{2,1,0:T(8,128)}), f32[16,128,128]{2,1,0:T(8,128)}) %all-gather.3.cloned.1.call-update) | async-done | bytes 1048592 | tf_op jit(solution)/shard_map/all_gather | solution.py:33
  207.4 1.3 reduce_sum.9
  208.7 0.1 copy.45
  208.9 46.9 %custom-call.8 = f32[4,128,128]{2,1,0:T(8,128)S(1)} custom-call(f32[4,128,128]{2,1,0:T(8,128)S(1)} %fusion.23), custom_call_target="Cholesky" | custom-call | tf_op jit(solution)/shard_map/jit(cholesky)/cholesky | solution.py:34
  255.9 0.1 compare_reduce_fusion
  256.0 0.8 multiply_bitcast_fusion
  256.8 39.3 %custom-call.9 = f32[4,1,128,128]{2,3,1,0:T(8,128)S(1)} custom-call(f32[4,1,128,128]{3,2,1,0:T(8,128)S(1)} %get-tuple-element.3), custom_call_target="InvertDiagBlocksLowerTriangular" | custom-call | tf_op jit(solution)/shard_map/jit(_solve_triangular)/vmap()/triangular_solve | solution.py:35
  296.1 2.8 fusion.4
  (17 shorter events, 0.2 us)
Async XLA Ops:
  7.2 1.2 copy-start
  8.4 9.5 %copy-start.3 = (s32[8,4]{0,1:T(4,128)S(1)}, s32[8,4]{0,1:T(4,128)}, u32[]{:S(2)}) copy-start(s32[8,4]{0,1:T(4,128)} %param.7) | copy-start | bytes 388
  12.7 20.6 %all-to-all-start = ((bf16[2,1,2048,128]{3,0,1,2:T(2,128)(2,1)}), bf16[2,1,2048,128]{3,0,1,2:T(2,128)(2,1)S(1)}, u32[]{:S(2)}, u32[]{:S(2)}) async-start(bf16[2,1,2048,128]{3,0,1,2:T(2,128)(2,1)} %copy.39), calls=%async_computation | async-start | bytes 2097152 | tf_op jit(solution)/shard_map/all_to_all | solution.py:19
  17.9 157.4 %reduce-scatter.2.cloned.1.call-start = ((), (), s32[]{:S(2)}) async-start(), calls=%async_computation.3 | async-start | bytes 5242880 | tf_op jit(solution)/shard_map/reduce_scatter | solution.py:31
  90.6 2.2 copy-start.2
  99.0 108.4 %all-gather.3.cloned.1.call-start = ((), (), s32[]{:S(2)}) async-start(), calls=%async_computation.4 | async-start | bytes 1310720 | tf_op jit(solution)/shard_map/all_gather | solution.py:33
  175.3 120.8 %copy-start.1 = (f32[4,512,128]{1,2,0:T(8,128)S(1)}, f32[4,512,128]{1,2,0:T(8,128)}, u32[]{:S(2)}) copy-start(f32[4,512,128]{1,2,0:T(8,128)} %reduce-scatter.2.cloned.1.call-done) | copy-start | bytes 3145732
Sparse Core Ops, SparseCore 0:
  99.1 76.1 reduce-scatter.1
  178.9 28.4 all-gather.2
